TPU v7x, 128 devices: a whole 4x4x4 slice. The times are simulated.
128 devices in a mesh: dp: 8 (over y_hi, x), mp: 16 (over z, y_lo, core).
Axes of the slice: x: 4, y: 4 (y_hi: 2, y_lo: 2; y = y_hi * 2 + y_lo), z: 4, core: 2. Of those that a mesh axis runs over, the one named last changes fastest.
Arguments:
- tokens: bfloat16 [6144, 16384], P('dp', 'mp'), may hold values from -6 to 6
- cotangent: bfloat16 [6144, 16384], P('dp', 'mp'), may hold values from -6 to 6
- blocks_w: bfloat16 [16, 5, 1024, 1024], P('mp'), may hold values from -0.078125 to 0.078125
- lowrank_u: bfloat16 [16384, 256], P('mp'), may hold values from -0.046875 to 0.046875
- lowrank_v: bfloat16 [256, 16384], P(None, 'mp'), may hold values from -0.375 to 0.375
Outputs:
- grad_tokens: float32 [6144, 16384], P('dp', 'mp')
- grad_blocks: float32 [1024, 16, 5, 1024], P('dp', 'mp')
- grad_u: float32 [16384, 256], P(('mp', 'dp'))
- grad_v: float32 [256, 16384], P(None, ('mp', 'dp'))
All inputs are finite; a program needn't handle non-finite values.
Results may differ from a plain program's by a relative error of at most 0.0029.
Values may be sent and summed in bfloat16 or wider, within the bound.
A program may use at most 192 MiB of HBM per device.

v0:
```python
import math

import jax
import jax.numpy as jnp
from jax import lax
from jax.sharding import PartitionSpec as P

FACT = 4


def partner(block, axis, apart):
    count = lax.axis_size(axis)
    route = []
    for low in range(count):
        high = low | 1 << apart
        if high != low and high < count:
            route += [(low, high), (high, low)]
    return lax.ppermute(block, axis, route)


def per_device(tokens, cotangent, blocks_w, lowrank_u, lowrank_v):
    local_blocks = blocks_w.shape[0]
    block_width = blocks_w.shape[2]
    tok_rows = tokens.shape[0]
    dp_count = lax.axis_size("dp")
    grad_scale = 1.0 / math.sqrt(tok_rows * dp_count)
    tok_blocks = tokens.reshape(tok_rows, local_blocks, block_width)
    cot_blocks = cotangent.reshape(tok_rows, local_blocks, block_width)
    low_part = jnp.dot(tokens, lowrank_u, preferred_element_type=jnp.float32)
    back_part = jnp.einsum("td,rd->tr", cotangent, lowrank_v, preferred_element_type=jnp.float32)
    low_sum, back_sum = lax.psum((low_part, back_part), "mp")
    low_in = low_sum.astype(jnp.bfloat16)
    low_back = back_sum.astype(jnp.bfloat16)
    grad_in = jnp.einsum("tr,dr->td", low_back, lowrank_u, preferred_element_type=jnp.float32)
    grad_in = grad_in.reshape(tok_rows, local_blocks, block_width)
    grad_in = grad_in + jnp.einsum(
        "tbo,bio->tbi", cot_blocks, blocks_w[:, 0], preferred_element_type=jnp.float32
    )
    sources = [tok_blocks]
    for factor in range(FACT):
        distance = 1 << factor
        outgoing = jnp.einsum(
            "tbo,bio->tbi", cot_blocks, blocks_w[:, factor + 1], preferred_element_type=jnp.float32
        )
        bit_index = (distance // local_blocks).bit_length() - 1
        partner_tokens = partner(tok_blocks, "mp", bit_index)
        partner_term = partner(outgoing, "mp", bit_index)
        grad_in = grad_in + partner_term
        sources.append(partner_tokens)
    grad_tokens = grad_in.reshape(tok_rows, local_blocks * block_width)
    stacked = jnp.stack(sources, axis=2)
    summed = lax.psum_scatter(
        jnp.einsum("tbsi,tbo->ibso", stacked, cot_blocks, preferred_element_type=jnp.float32),
        "dp",
        scatter_dimension=0,
        tiled=True,
    )
    grad_blocks = summed * grad_scale
    u_term = jnp.einsum("td,tr->dr", tokens, low_back, preferred_element_type=jnp.float32)
    v_term = jnp.einsum("tr,td->rd", low_in, cotangent, preferred_element_type=jnp.float32)
    grad_u, grad_v = (
        lax.psum_scatter(u_term, "dp", scatter_dimension=0, tiled=True),
        lax.psum_scatter(v_term, "dp", scatter_dimension=1, tiled=True),
    )
    return (grad_tokens, grad_blocks, grad_u * grad_scale, grad_v * grad_scale)


def solution(mesh):
    in_specs = (
        P("dp", "mp"),
        P("dp", "mp"),
        P("mp", None, None, None),
        P("mp", None),
        P(None, "mp"),
    )
    out_specs = (
        P("dp", "mp"),
        P("dp", "mp", None, None),
        P(("mp", "dp"), None),
        P(None, ("mp", "dp")),
    )
    return jax.shard_map(
        per_device, mesh=mesh, in_specs=in_specs, out_specs=out_specs, check_vma=False
    )
```

profile of v0, /device:TPU:0, one launch (start us, length us, event | category | flops | bytes accessed | tf_op | source)
XLA Modules:
  0.0 486.0 jit_solution(10054308702541622697)
XLA Ops:
  7.2 0.0 copy-start
  7.2 0.0 reduce-scatter.6.cloned.1.call-start
  7.2 1.3 copy-done
  8.6 2.6 fusion.38
  11.2 1.5 fusion.39
  12.6 73.0 %all-reduce.2 = (bf16[768,256]{1,0:T(8,128)(2,1)S(1)}, bf16[768,256]{1,0:T(8,128)(2,1)}) all-reduce(f32[768,256]{1,0:T(8,128)} %fusion.38, f32[768,256]{1,0:T(8,128)} %fusion.39), channel_id=1, replica_groups=mesh['dp'=8,'mp'=16] {'mp'}, use_global_device_ids=true, to_apply=%region_0.0 | all-reduce | flops 393216 | bytes 2359296 | tf_op jit(solution)/shard_map/psum | solution.py:31
  85.6 1.6 convolution_bitcast_fusion.1
  87.2 0.0 reduce-scatter.6.cloned.1.call-update
  87.3 0.0 reduce-scatter.8.cloned.1.call-start
  87.3 1.6 copy.14
  88.9 0.0 collective-permute-start.4
  88.9 0.0 collective-permute-start.5
  88.9 0.1 collective-permute-start.6
  89.0 2.1 collective-permute-start.7
  91.1 2.6 fusion.40
  93.7 0.0 reduce-scatter.8.cloned.1.call-update
  93.7 0.0 reduce-scatter.4.cloned.1.call-start
  93.8 0.1 bitcast_dynamic-update-slice_fusion.4
  93.9 1.5 bitcast_dynamic-update-slice_fusion.3
  95.4 35.8 %collective-permute-done.5 = bf16[768,1,1024]{0,2,1:T(8,128)(2,1)} collective-permute-done((bf16[768,1,1024]{0,2,1:T(8,128)(2,1)}, bf16[768,1,1024]{0,2,1:T(8,128)(2,1)}, u32[]{:S(2)}, u32[]{:S(2)}) %collective-permute-start.5) | collective-permute-done | bytes 1572896 | tf_op jit(solution)/shard_map/ppermute | solution.py:18
  131.2 1.5 bitcast_dynamic-update-slice_fusion.2
  132.7 0.0 collective-permute-done.6
  132.7 1.5 bitcast_dynamic-update-slice_fusion.1
  134.2 24.9 %collective-permute-done.7 = bf16[768,1,1024]{0,2,1:T(8,128)(2,1)} collective-permute-done((bf16[768,1,1024]{0,2,1:T(8,128)(2,1)}, bf16[768,1,1024]{0,2,1:T(8,128)(2,1)}, u32[]{:S(2)}, u32[]{:S(2)}) %collective-permute-start.7) | collective-permute-done | bytes 1572896 | tf_op jit(solution)/shard_map/ppermute | solution.py:18
  159.2 1.5 bitcast_dynamic-update-slice_fusion
  160.7 11.6 %convolution_bitcast_fusion = f32[1024,1,5,1024]{3,0,2,1:T(8,128)} fusion(bf16[768,1,5,1024]{0,3,2,1:T(8,128)(2,1)S(1)} %bitcast_dynamic-update-slice_fusion, bf16[768,1024]{1,0:T(8,128)(2,1)S(1)} %copy-done), kind=kOutput, calls=%fused_computation | convolution fusion | flops 8053063680 | bytes 30408704 | tf_op jit(solution)/shard_map/tbsi,tbo->ibso/dot_general | solution.py:53
  172.3 0.0 reduce-scatter.4.cloned.1.call-update
  172.3 0.0 slice-start
  172.3 0.0 slice-start.1
  172.4 5.2 %fusion.21 = f32[768,1,1024]{2,0,1:T(8,128)} fusion(bf16[768,1024]{1,0:T(8,128)(2,1)S(1)} %copy-done, bf16[1,5,1024,1024]{3,2,1,0:T(8,128)(2,1)} %param.7), kind=kOutput, calls=%fused_computation.23 | convolution fusion | flops 1610612736 | bytes 6815744 | tf_op jit(solution)/shard_map/tbo,bio->tbi/dot_general | solution.py:42
  177.5 5.2 %fusion.24 = f32[768,1,1024]{2,0,1:T(8,128)} fusion(bf16[768,1024]{1,0:T(8,128)(2,1)S(1)} %copy-done, bf16[1,5,1024,1024]{3,2,1,0:T(8,128)(2,1)} %param.7), kind=kOutput, calls=%fused_computation.24 | convolution fusion | flops 1610612736 | bytes 6815744 | tf_op jit(solution)/shard_map/tbo,bio->tbi/dot_general | solution.py:42
  182.8 0.4 collective-permute-start.1
  183.2 3.5 fusion.27
  186.7 1.5 collective-permute-start.2
  188.2 3.5 fusion.30
  191.7 4.6 collective-permute-start.3
  196.2 3.5 fusion.14
  199.7 0.9 broadcast_multiply_fusion.2
  200.6 0.8 copy.17
  201.4 35.2 %reduce-scatter.8.cloned.1.call-done = f32[256,128]{1,0:T(8,128)} async-done(((f32[256,1024]{1,0:T(8,128)}), f32[256,128]{1,0:T(8,128)}) %reduce-scatter.8.cloned.1.call-update) | async-done | bytes 131088 | tf_op jit(solution)/shard_map/reduce_scatter | solution.py:63
  236.6 1.6 broadcast_multiply_fusion.1
  238.1 28.1 %collective-permute-done.1 = f32[768,1,1024]{2,0,1:T(8,128)} collective-permute-done((f32[768,1,1024]{2,0,1:T(8,128)}, f32[768,1,1024]{2,0,1:T(8,128)}, u32[]{:S(2)}, u32[]{:S(2)}) %collective-permute-start.1) | collective-permute-done | bytes 3145760 | tf_op jit(solution)/shard_map/ppermute | solution.py:18
  266.2 0.0 collective-permute-done.2
  266.2 62.3 %collective-permute-done.3 = f32[768,1,1024]{2,0,1:T(8,128)} collective-permute-done((f32[768,1,1024]{2,0,1:T(8,128)}, f32[768,1,1024]{2,0,1:T(8,128)}, u32[]{:S(2)}, u32[]{:S(2)}) %collective-permute-start.3) | collective-permute-done | bytes 3145760 | tf_op jit(solution)/shard_map/ppermute | solution.py:18
  328.5 9.0 %fusion.5 = f32[768,1024]{1,0:T(8,128)} fusion(f32[768,1,1024]{2,0,1:T(8,128)} %collective-permute-done.3, f32[768,1,1024]{2,0,1:T(8,128)} %collective-permute-done.2, f32[768,1,1024]{2,0,1:T(8,128)} %collective-permute-done.1, f32[768,1,1024]{2,0,1:T(8,128)} %collective-permute-done, f32[1024,768]{0,1:T(8,128)} %fusion.14, ...), kind=kOutput, calls=%fused_computation.7 | convolution fusion | flops 406585344 | bytes 19791872 | tf_op jit(solution)/shard_map/tr,dr->td/dot_general | solution.py:34
  337.6 135.7 %reduce-scatter.4.cloned.1.call-done = f32[128,1,5,1024]{3,0,2,1:T(8,128)} async-done(((f32[1024,1,5,1024]{3,0,2,1:T(8,128)}), f32[128,1,5,1024]{3,0,2,1:T(8,128)}) %reduce-scatter.4.cloned.1.call-update) | async-done | bytes 2621456 | tf_op jit(solution)/shard_map/reduce_scatter | solution.py:52
  473.3 2.0 broadcast_multiply_fusion
  475.3 4.2 copy.16
  (17 shorter events, 0.0 us)
Async XLA Ops:
  7.2 1.4 copy-start
  7.2 4.0 copy-start.1
  7.2 192.5 %reduce-scatter.6.cloned.1.call-start = ((), (), s32[]{:S(2)}) async-start(), calls=%async_computation.4 | async-start | bytes 1179648 | tf_op jit(solution)/shard_map/reduce_scatter | solution.py:62
  8.6 2.6 copy-start.3
  87.3 149.3 %reduce-scatter.8.cloned.1.call-start = ((), (), s32[]{:S(2)}) async-start(), calls=%async_computation.5 | async-start | bytes 1179648 | tf_op jit(solution)/shard_map/reduce_scatter | solution.py:63
  88.9 4.9 %copy-start.2 = (bf16[768,1024]{0,1:T(8,128)(2,1)S(1)}, bf16[768,1024]{0,1:T(8,128)(2,1)}, u32[]{:S(2)}) copy-start(bf16[768,1024]{0,1:T(8,128)(2,1)} %copy.14) | copy-start | bytes 4718596
  88.9 5.0 %collective-permute-start.4 = (bf16[768,1,1024]{0,2,1:T(8,128)(2,1)}, bf16[768,1,1024]{0,2,1:T(8,128)(2,1)}, u32[]{:S(2)}, u32[]{:S(2)}) collective-permute-start(bf16[768,1,1024]{0,2,1:T(8,128)(2,1)} %bitcast.97), channel_id=1, source_target_pairs={{0,1},{1,0},{2,3},{3,2},{4,5},{5,4},{6,7},{7,6},{8,9},{9,8},{10,11... | collective-permute-start | bytes 4718600 | tf_op jit(solution)/shard_map/ppermute | solution.py:18
  88.9 42.3 %collective-permute-start.5 = (bf16[768,1,1024]{0,2,1:T(8,128)(2,1)}, bf16[768,1,1024]{0,2,1:T(8,128)(2,1)}, u32[]{:S(2)}, u32[]{:S(2)}) collective-permute-start(bf16[768,1,1024]{0,2,1:T(8,128)(2,1)} %bitcast.98), channel_id=1, source_target_pairs={{0,2},{2,0},{1,3},{3,1},{4,6},{6,4},{5,7},{7,5},{8,10},{10,8},{9,1... | collective-permute-start | bytes 4718600 | tf_op jit(solution)/shard_map/ppermute | solution.py:18
  88.9 43.8 %collective-permute-start.6 = (bf16[768,1,1024]{0,2,1:T(8,128)(2,1)}, bf16[768,1,1024]{0,2,1:T(8,128)(2,1)}, u32[]{:S(2)}, u32[]{:S(2)}) collective-permute-start(bf16[768,1,1024]{0,2,1:T(8,128)(2,1)} %bitcast.99), channel_id=1, source_target_pairs={{0,4},{4,0},{1,5},{5,1},{2,6},{6,2},{3,7},{7,3},{8,12},{12,8},{9,1... | collective-permute-start | bytes 4718600 | tf_op jit(solution)/shard_map/ppermute | solution.py:18
  89.0 70.2 %collective-permute-start.7 = (bf16[768,1,1024]{0,2,1:T(8,128)(2,1)}, bf16[768,1,1024]{0,2,1:T(8,128)(2,1)}, u32[]{:S(2)}, u32[]{:S(2)}) collective-permute-start(bf16[768,1,1024]{0,2,1:T(8,128)(2,1)} %bitcast.100), channel_id=1, source_target_pairs={{0,8},{8,0},{1,9},{9,1},{2,10},{10,2},{3,11},{11,3},{4,12},{12,4},... | collective-permute-start | bytes 4718600 | tf_op jit(solution)/shard_map/ppermute | solution.py:18
  93.7 379.5 %reduce-scatter.4.cloned.1.call-start = ((), (), s32[]{:S(2)}) async-start(), calls=%async_computation.3 | async-start | bytes 23592960 | tf_op jit(solution)/shard_map/reduce_scatter | solution.py:52
  172.3 10.9 %slice-start = ((s8[10485760]{0:T(1024)(128)(4,1)}), s8[4194304]{0:T(1024)(128)(4,1)S(1)}, s32[]{:S(2)}) async-start(s8[10485760]{0:T(1024)(128)(4,1)} %bitcast.101), calls=%async_computation.6 | async-start | bytes 8388608
  172.3 10.9 %slice-start.1 = ((s8[10485760]{0:T(1024)(128)(4,1)}), s8[4194304]{0:T(1024)(128)(4,1)S(1)}, s32[]{:S(2)}) async-start(s8[10485760]{0:T(1024)(128)(4,1)} %bitcast.101), calls=%async_computation.7 | async-start | bytes 8388608
  177.5 5.7 %slice-start.2 = ((s8[10485760]{0:T(1024)(128)(4,1)}), s8[2097152]{0:T(1024)(128)(4,1)S(1)}, s32[]{:S(2)}) async-start(s8[10485760]{0:T(1024)(128)(4,1)} %bitcast.101), calls=%async_computation.8 | async-start | bytes 4194304
  177.5 60.6 %collective-permute-start = (f32[768,1,1024]{2,0,1:T(8,128)}, f32[768,1,1024]{2,0,1:T(8,128)}, u32[]{:S(2)}, u32[]{:S(2)}) collective-permute-start(f32[768,1,1024]{2,0,1:T(8,128)} %fusion.21), channel_id=1, source_target_pairs={{0,1},{1,0},{2,3},{3,2},{4,5},{5,4},{6,7},{7,6},{8,9},{9,8},{10,11... | collective-permute-start | bytes 9437192 | tf_op jit(solution)/shard_map/ppermute | solution.py:18
  182.8 83.4 %collective-permute-start.1 = (f32[768,1,1024]{2,0,1:T(8,128)}, f32[768,1,1024]{2,0,1:T(8,128)}, u32[]{:S(2)}, u32[]{:S(2)}) collective-permute-start(f32[768,1,1024]{2,0,1:T(8,128)} %fusion.24), channel_id=1, source_target_pairs={{0,2},{2,0},{1,3},{3,1},{4,6},{6,4},{5,7},{7,5},{8,10},{10,8},{9,1... | collective-permute-start | bytes 9437192 | tf_op jit(solution)/shard_map/ppermute | solution.py:18
  186.7 79.5 %collective-permute-start.2 = (f32[768,1,1024]{2,0,1:T(8,128)}, f32[768,1,1024]{2,0,1:T(8,128)}, u32[]{:S(2)}, u32[]{:S(2)}) collective-permute-start(f32[768,1,1024]{2,0,1:T(8,128)} %fusion.27), channel_id=1, source_target_pairs={{0,4},{4,0},{1,5},{5,1},{2,6},{6,2},{3,7},{7,3},{8,12},{12,8},{9,1... | collective-permute-start | bytes 9437192 | tf_op jit(solution)/shard_map/ppermute | solution.py:18
  191.7 136.9 %copy-start.4 = (bf16[1024,256]{1,0:T(8,128)(2,1)S(1)}, bf16[1024,256]{1,0:T(8,128)(2,1)}, u32[]{:S(2)}) copy-start(bf16[1024,256]{1,0:T(8,128)(2,1)} %param.8) | copy-start | bytes 1572868
  191.7 136.8 %collective-permute-start.3 = (f32[768,1,1024]{2,0,1:T(8,128)}, f32[768,1,1024]{2,0,1:T(8,128)}, u32[]{:S(2)}, u32[]{:S(2)}) collective-permute-start(f32[768,1,1024]{2,0,1:T(8,128)} %fusion.30), channel_id=1, source_target_pairs={{0,8},{8,0},{1,9},{9,1},{2,10},{10,2},{3,11},{11,3},{4,12},{12,4},... | collective-permute-start | bytes 9437192 | tf_op jit(solution)/shard_map/ppermute | solution.py:18
Sparse Core Ops, SparseCore 0:
  87.4 71.7 reduce-scatter.5
  163.3 73.2 reduce-scatter.7
  240.6 232.6 reduce-scatter.3
where the time goes:
time: 486 us
  waiting for transfers between devices  322 us (66%)
  blocking collectives  73 us (15%)
  matrix products  49.8 us (10%)
  local copies, waits for them, and re-layouts  14 us (3%)
  between operations  13.9 us (3%)
  starting transfers between devices  8.81 us (2%)
    ppermute x8, waiting for transfers between devices, partner(): return lax.ppermute(block, axis, route)  151 us
    reduce_scatter x1, waiting for transfers between devices, per_device(): lax.psum_scatter(jnp.einsum('tbsi,tbo->ibso', stacked, cot_blocks, prefer...  136 us
    psum x1, blocking collectives, per_device(): low_sum, back_sum = lax.psum((low_part, back_part), 'mp')  73 us
    reduce_scatter x1, waiting for transfers between devices, per_device(): lax.psum_scatter(v_term, 'dp', scatter_dimension=1, tiled=True)  35.2 us
    dot_general x4, matrix products, per_device(): jnp.einsum('tbo,bio->tbi', cot_blocks, blocks_w[:, factor + 1], preferred...  17.4 us
    unnamed x23, local copies, waits for them, and re-layouts  12.5 us
    dot_general x1, matrix products, per_device(): jnp.einsum('tbsi,tbo->ibso', stacked, cot_blocks, preferred_element_type=...  11.6 us
  transfers between devices with their start and end apart: 11, of which 6 were waited for; matrix products, arithmetic and copies ran while one was open for 11% of the time, Pallas kernels for 0%

commit v1 on v0

v1 whole, which is shorter than its diff:
```python
import functools
import math

import jax
import jax.numpy as jnp
from jax import lax
from jax.experimental import pallas as pl
from jax.experimental.pallas import tpu as pltpu
from jax.sharding import PartitionSpec as P

MESH = pl.DeviceIdType.MESH
F32 = jnp.float32
BF16 = jnp.bfloat16
CHUNKS = 4


def flip(value, bit):
    return value + bit - 2 * bit * lax.rem(lax.div(value, bit), 2)


def dot_nt(a, b):
    return lax.dot_general(a, b, (((1,), (1,)), ((), ())), preferred_element_type=F32)


def dot_tn(a, b):
    return lax.dot_general(a, b, (((0,), (0,)), ((), ())), preferred_element_type=F32)


def kernel(
    rows, blk, rank, scale,
    tok_hbm, cot_hbm, w_hbm, u_hbm, v_hbm,
    gt_hbm, gb_hbm, gu_ref, gv_ref,
    tq, cx, tx, w, uu, vv,
    s4, s34, s2, s1, r4, r34, r2, r1,
    acc, ps, pr, gt,
    lp, lr1, lr2, lz, lr3, lf,
    eb, er, eo, eyu, eyv,
    lsem, ssem, rsem,
):
    qw = blk // 8
    dp = lax.axis_index("dp")
    mp = lax.axis_index("mp")
    x = lax.rem(dp, 4)
    yh = lax.div(dp, 4)
    core = lax.rem(mp, 2)
    z = lax.div(mp, 4)

    def px(rel):
        return (yh * 4 + lax.rem(x + rel, 4), mp)

    m1 = (dp, flip(mp, 1))
    m2 = (dp, flip(mp, 2))
    m4 = (dp, flip(mp, 4))
    m8 = (dp, flip(mp, 8))
    m12 = (dp, flip(flip(mp, 4), 8))
    yy = (flip(dp, 4), mp)

    nl = [0]

    def load(src, dst):
        cp = pltpu.make_async_copy(src, dst, lsem.at[nl[0]])
        nl[0] += 1
        cp.start()
        return cp

    own = []
    tl = []
    for h in range(2):
        own.append(load(
            tok_hbm.at[:, pl.ds(pl.multiple_of(h * 4 * qw + x * qw, qw), qw)],
            tx.at[0, 0, :, pl.ds(h * qw, qw)],
        ))
    for q in range(4):
        for h in range(2):
            tl.append(load(
                tok_hbm.at[:, pl.ds(h * 4 * qw + q * qw, qw)],
                tq.at[q, :, pl.ds(h * qw, qw)],
            ))
    cl = load(cot_hbm, cx.at[0])
    ul = load(u_hbm, uu)
    vl = load(v_hbm, vv)
    wl = {s: load(w_hbm.at[s], w.at[s]) for s in (4, 3, 2, 1, 0)}

    barrier = pltpu.get_barrier_semaphore()
    peers = [px(1), px(3), px(2), m1, m2, m4, m8, m12, yy]
    for peer in peers:
        pl.semaphore_signal(barrier, 1, device_id=peer, device_id_type=MESH)
    pl.semaphore_wait(barrier, len(peers))

    ns = [0]
    sent = []

    def send(src, dst, peer):
        k = ns[0]
        ns[0] += 1
        cp = pltpu.make_async_remote_copy(
            src_ref=src, dst_ref=dst, send_sem=ssem.at[k], recv_sem=rsem.at[k],
            device_id=peer, device_id_type=MESH,
        )
        cp.start()
        sent.append(cp)
        return k, peer

    def recv(key, dst):
        k, peer = key
        pltpu.make_async_remote_copy(
            src_ref=dst, dst_ref=dst, send_sem=ssem.at[k], recv_sem=rsem.at[k],
            device_id=peer, device_id_type=MESH,
        ).wait_recv()

    for cp in tl:
        cp.wait()
    xt = {}
    for rel in (1, 3, 2):
        slot = (4 - rel) % 4
        xt[slot] = send(tq.at[lax.rem(x + rel, 4)], tx.at[0, slot], px(rel))
    for cp in own:
        cp.wait()
    tm = {}

    def spread(slot):
        tm[3, slot] = send(tx.at[0, slot], tx.at[3, slot], m4)
        tm[2, slot] = send(tx.at[0, slot], tx.at[2, slot], m2)
        tm[1, slot] = send(tx.at[0, slot], tx.at[1, slot], m1)

    def onward(slot):
        recv(tm[3, slot], tx.at[3, slot])
        tm[4, slot] = send(tx.at[3, slot], tx.at[4, slot], m12)

    spread(0)
    cl.wait()
    half = rows // 2
    lo, hi = pl.ds(0, half), pl.ds(half, half)
    xc = {}
    xc[3, 0] = send(cx.at[0, lo], cx.at[3, lo], px(1))
    xc[1, 1] = send(cx.at[0, hi], cx.at[1, hi], px(3))
    xc[3, 1] = send(cx.at[0, hi], cx.at[3, hi], px(1))
    xc[1, 0] = send(cx.at[0, lo], cx.at[1, lo], px(3))

    ul.wait()
    vl.wait()
    low = jnp.zeros((rows, rank), F32)
    for q in range(4):
        uq = jnp.concatenate(
            [uu[q * qw:(q + 1) * qw, :], uu[(4 + q) * qw:(5 + q) * qw, :]], axis=0
        )
        low = low + jnp.dot(tq[q], uq, preferred_element_type=F32)
    lp[:, 0:rank] = low
    lp[:, rank:2 * rank] = dot_nt(cx[0], vv[...])
    hr = rows // 2
    a1 = send(lp.at[pl.ds(pl.multiple_of((1 - core) * hr, hr), hr)], lr1, m1)

    tile = blk // 4

    def term(slot, out, first, count, extra=None):
        at = pl.ds(first, count)

        def step(n, carry):
            cols = pl.ds(pl.multiple_of(n * tile, tile), tile)
            value = dot_nt(cx[0, at, :], w[slot, cols, :])
            if extra is not None:
                value = value + extra[at, cols].astype(F32)
            out[at, cols] = value.astype(BF16)
            return carry

        lax.fori_loop(0, 4, step, 0)

    cr = rows // CHUNKS
    wl[4].wait()
    t4 = []
    for c in range(CHUNKS):
        term(4, s4, c * cr, cr)
        at = pl.ds(c * cr, cr)
        t4.append(send(s4.at[at], r4.at[at], m12))
        if c == 1:
            recv(a1, lr1)
            mine = pl.ds(pl.multiple_of(core * hr, hr), hr)
            lr1[...] = lr1[...] + lp[mine, :]
            zr = hr // 4
            a2 = {}
            for v, peer in ((1, m4), (3, m12), (2, m8)):
                zz = z
                if v & 1:
                    zz = flip(zz, 1)
                if v & 2:
                    zz = flip(zz, 2)
                a2[v] = send(
                    lr1.at[pl.ds(pl.multiple_of(zz * zr, zr), zr)], lr2.at[v - 1], peer
                )
    onward(0)
    for slot in (3, 1):
        recv(xt[slot], tx.at[0, slot])
        spread(slot)
    for v in (1, 3, 2):
        recv(a2[v], lr2.at[v - 1])
    lz[...] = (
        lr1[pl.ds(pl.multiple_of(z * zr, zr), zr), :] + lr2[0] + lr2[1] + lr2[2]
    )
    a3 = send(lz, lr3, m2)
    recv(xt[2], tx.at[0, 2])
    spread(2)
    wl[2].wait()
    term(2, s2, 0, rows)
    t2 = send(s2, r2, m2)
    wl[1].wait()
    term(1, s1, 0, rows)
    t1 = send(s1, r1, m1)
    onward(3)
    onward(1)
    recv(a3, lr3)
    piece = pl.ds(pl.multiple_of(core * hr + z * zr, zr), zr)
    lf[piece, :] = (lz[...] + lr3[...]).astype(BF16)
    a4 = {}
    for v, peer in ((1, m4), (3, m12), (2, m8)):
        a4[v] = send(lf.at[piece], lf.at[piece], peer)
    wl[3].wait()
    t34 = []

    def chain(c):
        at = pl.ds(c * cr, cr)
        recv(t4[c], r4.at[at])
        term(3, s34, c * cr, cr, r4)
        t34.append(send(s34.at[at], r34.at[at], m4))

    chain(0)
    chain(1)
    onward(2)
    recv(xc[3, 0], cx.at[3, lo])
    xf0 = send(cx.at[3, lo], cx.at[2, lo], px(1))
    recv(xc[1, 1], cx.at[1, hi])
    xf1 = send(cx.at[1, hi], cx.at[2, hi], px(3))
    chain(2)
    for v in (1, 3, 2):
        zz = z
        if v & 1:
            zz = flip(zz, 1)
        if v & 2:
            zz = flip(zz, 2)
        recv(a4[v], lf.at[pl.ds(pl.multiple_of(core * hr + zz * zr, zr), zr)])
    mine = pl.ds(pl.multiple_of(core * hr, hr), hr)
    other = pl.ds(pl.multiple_of((1 - core) * hr, hr), hr)
    a5 = send(lf.at[mine], lf.at[mine], m1)
    chain(3)

    wide = blk // 2

    def product(slot, first):
        def step(i, carry):
            s = lax.div(i, 2)
            cols = pl.ds(pl.multiple_of(lax.rem(i, 2) * wide, wide), wide)
            value = dot_tn(tx[s, slot], cx[slot, :, cols])
            if first:
                acc[s, :, cols] = value
            else:
                acc[s, :, cols] = acc[s, :, cols] + value
            return carry
        return step

    for s in (1, 2):
        recv(tm[s, 0], tx.at[s, 0])
    recv(tm[4, 0], tx.at[4, 0])
    lax.fori_loop(0, 10, product(0, True), 0)

    recv(a5, lf.at[other])
    ex = {}
    for rel in (1, 3, 2, 0):
        q = lax.rem(x + rel, 4)
        gu = dot_tn(tq[q], lf[:, rank:2 * rank])
        ga = dot_tn(lf[:, 0:rank], cx[0, :, pl.ds(pl.multiple_of(q * qw, qw), qw)])
        gb = dot_tn(lf[:, 0:rank], cx[0, :, pl.ds(pl.multiple_of(4 * qw + q * qw, qw), qw)])
        if rel == 0:
            eo[0:2 * qw, :] = gu
            eo[2 * qw:2 * qw + rank, 0:qw] = ga
            eo[2 * qw:2 * qw + rank, qw:2 * qw] = gb
        else:
            eb[rel - 1, 0:2 * qw, :] = gu.astype(BF16)
            eb[rel - 1, 2 * qw:2 * qw + rank, 0:qw] = ga.astype(BF16)
            eb[rel - 1, 2 * qw:2 * qw + rank, qw:2 * qw] = gb.astype(BF16)
            ex[rel] = send(eb.at[rel - 1], er.at[rel - 1], px(rel))

    recv(xc[3, 1], cx.at[3, hi])
    for s in (1, 2, 4):
        recv(tm[s, 3], tx.at[s, 3])
    lax.fori_loop(0, 10, product(3, False), 0)
    recv(xc[1, 0], cx.at[1, lo])
    for s in (1, 2, 4):
        recv(tm[s, 1], tx.at[s, 1])
    lax.fori_loop(0, 10, product(1, False), 0)
    for s in (1, 2, 4):
        recv(tm[s, 2], tx.at[s, 2])
    recv(xf0, cx.at[2, lo])
    recv(xf1, cx.at[2, hi])
    away = pl.ds(pl.multiple_of((1 - yh) * qw, qw), qw)
    home = pl.ds(pl.multiple_of(yh * qw, qw), qw)
    py = []
    last = product(2, False)
    for s in range(5):
        last(2 * s, 0)
        last(2 * s + 1, 0)
        ps[s] = acc[s, away, :].astype(BF16)
        py.append(send(ps.at[s], pr.at[s], yy))
    for rel in (1, 3, 2):
        recv(ex[rel], er.at[rel - 1])
        eo[...] = eo[...] + er[rel - 1].astype(F32)
    eu = send(eo.at[away], eyu, yy)
    ev = send(eo.at[pl.ds(2 * qw, rank), away], eyv, yy)

    recv(t1, r1)
    recv(t2, r2)
    for c in range(CHUNKS):
        recv(t34[c], r34.at[pl.ds(c * cr, cr)])
    wl[0].wait()

    def total(n, carry):
        cols = pl.ds(pl.multiple_of(n * tile, tile), tile)
        value = dot_nt(cx[0], w[0, cols, :])
        value = value + dot_nt(lf[:, rank:2 * rank], uu[cols, :])
        value = value + r1[:, cols].astype(F32)
        value = value + r2[:, cols].astype(F32)
        gt[:, cols] = value + r34[:, cols].astype(F32)
        return carry

    lax.fori_loop(0, 4, total, 0)
    outs = [load(gt, gt_hbm)]
    for s in range(5):
        recv(py[s], pr.at[s])
        acc[s, home, :] = (acc[s, home, :] + pr[s].astype(F32)) * scale
        outs.append(load(acc.at[s, home, :], gb_hbm.at[s]))
    recv(eu, eyu)
    recv(ev, eyv)
    gu_ref[...] = (eo[home, :] + eyu[...]) * scale
    gv_ref[...] = (eo[pl.ds(2 * qw, rank), home] + eyv[...]) * scale
    for cp in sent:
        cp.wait_send()
    for cp in outs:
        cp.wait()


def per_device(tokens, cotangent, blocks_w, lowrank_u, lowrank_v):
    rows, blk = tokens.shape
    rank = lowrank_u.shape[1]
    slots = blocks_w.shape[1]
    qw = blk // 8
    scale = 1.0 / math.sqrt(rows * lax.axis_size("dp"))
    big = (rows, blk)
    hr = rows // 2
    n_send = 60
    scratch = [
        pltpu.VMEM((4, rows, 2 * qw), BF16),
        pltpu.VMEM((4,) + big, BF16),
        pltpu.VMEM((slots, 4, rows, 2 * qw), BF16),
        pltpu.VMEM((slots, blk, blk), BF16),
        pltpu.VMEM((blk, rank), BF16),
        pltpu.VMEM((rank, blk), BF16),
    ]
    scratch += [pltpu.VMEM(big, BF16)] * 8
    scratch += [
        pltpu.VMEM((slots, 2 * qw, blk), F32),
        pltpu.VMEM((slots, qw, blk), BF16),
        pltpu.VMEM((slots, qw, blk), BF16),
        pltpu.VMEM(big, F32),
        pltpu.VMEM((rows, 2 * rank), F32),
        pltpu.VMEM((hr, 2 * rank), F32),
        pltpu.VMEM((3, hr // 4, 2 * rank), F32),
        pltpu.VMEM((hr // 4, 2 * rank), F32),
        pltpu.VMEM((hr // 4, 2 * rank), F32),
        pltpu.VMEM((rows, 2 * rank), BF16),
        pltpu.VMEM((3, 2 * qw + rank, rank), BF16),
        pltpu.VMEM((3, 2 * qw + rank, rank), BF16),
        pltpu.VMEM((2 * qw + rank, rank), F32),
        pltpu.VMEM((qw, rank), F32),
        pltpu.VMEM((rank, qw), F32),
        pltpu.SemaphoreType.DMA((32,)),
        pltpu.SemaphoreType.DMA((n_send,)),
        pltpu.SemaphoreType.DMA((n_send,)),
    ]
    anyspace = pl.BlockSpec(memory_space=pl.ANY)
    vmem = pl.BlockSpec(memory_space=pltpu.VMEM)
    gt, gb, gu, gv = pl.pallas_call(
        functools.partial(kernel, rows, blk, rank, scale),
        out_shape=(
            jax.ShapeDtypeStruct(big, F32),
            jax.ShapeDtypeStruct((slots, qw, blk), F32),
            jax.ShapeDtypeStruct((qw, rank), F32),
            jax.ShapeDtypeStruct((rank, qw), F32),
        ),
        in_specs=[anyspace] * 5,
        out_specs=(anyspace, anyspace, vmem, vmem),
        scratch_shapes=scratch,
        compiler_params=pltpu.CompilerParams(
            collective_id=0, has_side_effects=True, vmem_limit_bytes=64 << 20
        ),
        name="butterfly",
    )(tokens, cotangent, blocks_w[0], lowrank_u, lowrank_v)
    return gt, jnp.transpose(gb, (1, 0, 2))[:, None], gu, gv


def solution(mesh):
    in_specs = (
        P("dp", "mp"),
        P("dp", "mp"),
        P("mp", None, None, None),
        P("mp", None),
        P(None, "mp"),
    )
    out_specs = (
        P("dp", "mp"),
        P("dp", "mp", None, None),
        P(("mp", "dp"), None),
        P(None, ("mp", "dp")),
    )
    return jax.shard_map(
        per_device, mesh=mesh, in_specs=in_specs, out_specs=out_specs, check_vma=False
    )
```

time: 486 us -> 147 us (0.30)
  waiting for transfers between devices: 322 us -> 0 us
  Pallas kernels: 0 us -> 137 us
  blocking collectives: 73 us -> 0 us
  matrix products: 49.8 us -> 0 us
  between operations: 13.9 us -> 0.65 us
  starting transfers between devices: 8.81 us -> 0 us
  local copies, waits for them, and re-layouts: 14 us -> 9.06 us
    reduce_scatter x3 -> x0, waiting for transfers between devices: 171 us -> none  [the longest x1 136 us: per_device(): lax.psum_scatter(jnp.einsum('tbsi,tbo->ibso', stacked, cot_blocks, prefer...]
    ppermute x8 -> x0, waiting for transfers between devices: 151 us -> none  [partner(): return lax.ppermute(block, axis, route)]
    pallas_call x0 -> x1, Pallas kernels: none -> 137 us  [per_device(): pl.pallas_call(functools.partial(kernel, rows, blk, rank, scale), out_sha...]
    psum x1 -> x0, blocking collectives: 73 us -> none  [per_device(): low_sum, back_sum = lax.psum((low_part, back_part), 'mp')]
    dot_general x11 -> x0, matrix products: 49.8 us -> none  [the longest x4 17.4 us: per_device(): jnp.einsum('tbo,bio->tbi', cot_blocks, blocks_w[:, factor + 1], preferred...]
    ppermute x8 -> x0, starting transfers between devices: 8.69 us -> none  [partner(): return lax.ppermute(block, axis, route)]
    unnamed x23 -> x10, local copies, waits for them, and re-layouts: 12.5 us -> 9.06 us
  transfers between devices with their start and end apart: 11 -> 0, of which waited for: 6 -> 0; matrix products, arithmetic and copies ran while one was open for 11% -> 0% of each run, Pallas kernels for 0% -> 0%
where the time goes in v1:
time: 147 us
  Pallas kernels  137 us (93%)
  local copies, waits for them, and re-layouts  9.06 us (6%)
    pallas_call x1, Pallas kernels, per_device(): pl.pallas_call(functools.partial(kernel, rows, blk, rank, scale), out_sha...  137 us
    unnamed x10, local copies, waits for them, and re-layouts  9.06 us

profile of v1, /device:TPU:0, one launch (start us, length us, event | category | flops | bytes accessed | tf_op | source)
XLA Modules:
  0.0 146.6 jit_solution(2145310493403153210)
XLA Ops:
  0.6 136.9 %butterfly.1 = (f32[768,1024]{1,0:T(8,128)}, f32[5,128,1024]{2,1,0:T(8,128)}, f32[128,256]{1,0:T(8,128)}, f32[256,128]{1,0:T(8,128)}) custom-call(bf16[768,1024]{1,0:T(8,128)(2,1)} %tok_hbm.1, bf16[768,1024]{1,0:T(8,128)(2,1)} %cot_hbm.1, bf16[5,1024,1024]{2,1,0:T(8,128)(2,1)} %bitcast.4, bf16[1024,256]{1,0:T(8,128)(2,1)} %u_hbm.1, bf16[256,1024]{1,0:T(8,128)(2,1)} %v_hbm.1), custom_call_target="tpu_custom_call" | custom-call | tf_op jit(solution)/shard_map/butterfly/pallas_call | solution.py:379
  137.5 0.0 copy-start
  137.5 6.1 %copy.9 = f32[128,1,5,1024]{3,1,2,0:T(1,128)} copy(f32[128,1,5,1024]{3,0,2,1:T(8,128)} %bitcast.5) | data formatting | bytes 5242880
  143.6 0.0 copy-done
  143.6 0.0 copy-start.2
  143.6 0.0 copy-start.1
  143.6 1.7 %copy.13 = f32[768,1024]{1,0:T(8,128)} copy(f32[768,1024]{1,0:T(8,128)S(1)} %copy-done) | data formatting | bytes 6291456
  145.3 0.0 copy-done.2
  145.3 0.7 copy.14
  145.9 0.0 copy-done.1
  145.9 0.7 copy.15
Async XLA Ops:
  137.5 6.1 %copy-start = (f32[768,1024]{1,0:T(8,128)S(1)}, f32[768,1024]{1,0:T(8,128)}, u32[]{:S(2)}) copy-start(f32[768,1024]{1,0:T(8,128)} %get-tuple-element.20) | copy-start | bytes 9437188
  143.6 1.7 %copy-start.2 = (f32[128,256]{1,0:T(8,128)S(1)}, f32[128,256]{1,0:T(8,128)}, u32[]{:S(2)}) copy-start(f32[128,256]{1,0:T(8,128)} %get-tuple-element.22) | copy-start | bytes 393220
  143.6 2.3 %copy-start.1 = (f32[256,128]{1,0:T(8,128)S(1)}, f32[256,128]{1,0:T(8,128)}, u32[]{:S(2)}) copy-start(f32[256,128]{1,0:T(8,128)} %get-tuple-element.23) | copy-start | bytes 393220

commit v2 on v1

--- a/solution.py
+++ b/solution.py
@@ -32,9 +32,9 @@
     gt_hbm, gb_hbm, gu_ref, gv_ref,
     tq, cx, tx, w, uu, vv,
     s4, s34, s2, s1, r4, r34, r2, r1,
-    acc, ps, pr, gt,
+    acc, ps, pr, gt, gb,
     lp, lr1, lr2, lz, lr3, lf,
-    eb, er, eo, eyu, eyv,
+    eb, er, eo, su, sv, eyu, eyv,
     lsem, ssem, rsem,
 ):
     qw = blk // 8
@@ -63,6 +63,10 @@
         cp.start()
         return cp
 
+    barrier = pltpu.get_barrier_semaphore()
+    peers = [px(1), px(3), px(2), m1, m2, m4, m8, m12, yy]
+    for peer in peers:
+        pl.semaphore_signal(barrier, 1, device_id=peer, device_id_type=MESH)
     own = []
     tl = []
     for h in range(2):
@@ -79,12 +83,6 @@
     cl = load(cot_hbm, cx.at[0])
     ul = load(u_hbm, uu)
     vl = load(v_hbm, vv)
-    wl = {s: load(w_hbm.at[s], w.at[s]) for s in (4, 3, 2, 1, 0)}
-
-    barrier = pltpu.get_barrier_semaphore()
-    peers = [px(1), px(3), px(2), m1, m2, m4, m8, m12, yy]
-    for peer in peers:
-        pl.semaphore_signal(barrier, 1, device_id=peer, device_id_type=MESH)
     pl.semaphore_wait(barrier, len(peers))
 
     ns = [0]
@@ -108,26 +106,26 @@
             device_id=peer, device_id_type=MESH,
         ).wait_recv()
 
+    tm = {}
+
+    def spread(slot):
+        tm[3, slot] = send(tx.at[0, slot], tx.at[3, slot], m4)
+        tm[2, slot] = send(tx.at[0, slot], tx.at[2, slot], m2)
+        tm[1, slot] = send(tx.at[0, slot], tx.at[1, slot], m1)
+
+    def onward(slot):
+        recv(tm[3, slot], tx.at[3, slot])
+        tm[4, slot] = send(tx.at[3, slot], tx.at[4, slot], m12)
+
+    for cp in own:
+        cp.wait()
+    spread(0)
     for cp in tl:
         cp.wait()
     xt = {}
     for rel in (1, 3, 2):
         slot = (4 - rel) % 4
         xt[slot] = send(tq.at[lax.rem(x + rel, 4)], tx.at[0, slot], px(rel))
-    for cp in own:
-        cp.wait()
-    tm = {}
-
-    def spread(slot):
-        tm[3, slot] = send(tx.at[0, slot], tx.at[3, slot], m4)
-        tm[2, slot] = send(tx.at[0, slot], tx.at[2, slot], m2)
-        tm[1, slot] = send(tx.at[0, slot], tx.at[1, slot], m1)
-
-    def onward(slot):
-        recv(tm[3, slot], tx.at[3, slot])
-        tm[4, slot] = send(tx.at[3, slot], tx.at[4, slot], m12)
-
-    spread(0)
     cl.wait()
     half = rows // 2
     lo, hi = pl.ds(0, half), pl.ds(half, half)
@@ -136,6 +134,7 @@
     xc[1, 1] = send(cx.at[0, hi], cx.at[1, hi], px(3))
     xc[3, 1] = send(cx.at[0, hi], cx.at[3, hi], px(1))
     xc[1, 0] = send(cx.at[0, lo], cx.at[1, lo], px(3))
+    wl = {s: load(w_hbm.at[s], w.at[s]) for s in (4, 2, 3, 1, 0)}
 
     ul.wait()
     vl.wait()
@@ -148,7 +147,10 @@
     lp[:, 0:rank] = low
     lp[:, rank:2 * rank] = dot_nt(cx[0], vv[...])
     hr = rows // 2
-    a1 = send(lp.at[pl.ds(pl.multiple_of((1 - core) * hr, hr), hr)], lr1, m1)
+    zr = hr // 4
+    mine = pl.ds(pl.multiple_of(core * hr, hr), hr)
+    other = pl.ds(pl.multiple_of((1 - core) * hr, hr), hr)
+    a1 = send(lp.at[other], lr1, m1)
 
     tile = blk // 4
 
@@ -165,33 +167,66 @@
 
         lax.fori_loop(0, 4, step, 0)
 
+    def along(v):
+        zz = z
+        if v & 1:
+            zz = flip(zz, 1)
+        if v & 2:
+            zz = flip(zz, 2)
+        return zz
+
+    hops = ((1, m4), (3, m12), (2, m8))
     cr = rows // CHUNKS
     wl[4].wait()
     t4 = []
-    for c in range(CHUNKS):
+
+    def fourth(c):
         term(4, s4, c * cr, cr)
         at = pl.ds(c * cr, cr)
         t4.append(send(s4.at[at], r4.at[at], m12))
-        if c == 1:
-            recv(a1, lr1)
-            mine = pl.ds(pl.multiple_of(core * hr, hr), hr)
-            lr1[...] = lr1[...] + lp[mine, :]
-            zr = hr // 4
-            a2 = {}
-            for v, peer in ((1, m4), (3, m12), (2, m8)):
-                zz = z
-                if v & 1:
-                    zz = flip(zz, 1)
-                if v & 2:
-                    zz = flip(zz, 2)
-                a2[v] = send(
-                    lr1.at[pl.ds(pl.multiple_of(zz * zr, zr), zr)], lr2.at[v - 1], peer
-                )
-    onward(0)
+
+    fourth(0)
+    recv(a1, lr1)
+    lr1[...] = lr1[...] + lp[mine, :]
+    a2 = {}
+    for v, peer in hops:
+        a2[v] = send(
+            lr1.at[pl.ds(pl.multiple_of(along(v) * zr, zr), zr)], lr2.at[v - 1], peer
+        )
+    fourth(1)
+    t34 = []
+
+    def chain(c):
+        at = pl.ds(c * cr, cr)
+        recv(t4[c], r4.at[at])
+        term(3, s34, c * cr, cr, r4)
+        t34.append(send(s34.at[at], r34.at[at], m4))
+
+    wide = blk // 2
+
+    def product(slot, first):
+        def step(i, carry):
+            s = lax.div(i, 2)
+            cols = pl.ds(pl.multiple_of(lax.rem(i, 2) * wide, wide), wide)
+            value = dot_tn(tx[s, slot], cx[slot, :, cols])
+            if first:
+                acc[s, :, cols] = value
+            else:
+                acc[s, :, cols] = acc[s, :, cols] + value
+            return carry
+        return step
+
+
+    def multiply(slot, first):
+        for s in (1, 2, 4):
+            recv(tm[s, slot], tx.at[s, slot])
+        lax.fori_loop(0, 10, product(slot, first), 0)
+
     for slot in (3, 1):
         recv(xt[slot], tx.at[0, slot])
         spread(slot)
-    for v in (1, 3, 2):
+    onward(0)
+    for v, peer in hops:
         recv(a2[v], lr2.at[v - 1])
     lz[...] = (
         lr1[pl.ds(pl.multiple_of(z * zr, zr), zr), :] + lr2[0] + lr2[1] + lr2[2]
@@ -211,82 +246,45 @@
     piece = pl.ds(pl.multiple_of(core * hr + z * zr, zr), zr)
     lf[piece, :] = (lz[...] + lr3[...]).astype(BF16)
     a4 = {}
-    for v, peer in ((1, m4), (3, m12), (2, m8)):
+    for v, peer in hops:
         a4[v] = send(lf.at[piece], lf.at[piece], peer)
+    fourth(2)
     wl[3].wait()
-    t34 = []
-
-    def chain(c):
-        at = pl.ds(c * cr, cr)
-        recv(t4[c], r4.at[at])
-        term(3, s34, c * cr, cr, r4)
-        t34.append(send(s34.at[at], r34.at[at], m4))
-
-    chain(0)
-    chain(1)
-    onward(2)
     recv(xc[3, 0], cx.at[3, lo])
     xf0 = send(cx.at[3, lo], cx.at[2, lo], px(1))
     recv(xc[1, 1], cx.at[1, hi])
     xf1 = send(cx.at[1, hi], cx.at[2, hi], px(3))
+    chain(0)
+    chain(1)
+    onward(2)
+    fourth(3)
+    multiply(0, True)
+    recv(xc[3, 1], cx.at[3, hi])
+    multiply(3, False)
+    recv(xc[1, 0], cx.at[1, lo])
+    multiply(1, False)
+    for v, peer in hops:
+        recv(a4[v], lf.at[pl.ds(pl.multiple_of(core * hr + along(v) * zr, zr), zr)])
+    a5 = send(lf.at[mine], lf.at[mine], m1)
     chain(2)
-    for v in (1, 3, 2):
-        zz = z
-        if v & 1:
-            zz = flip(zz, 1)
-        if v & 2:
-            zz = flip(zz, 2)
-        recv(a4[v], lf.at[pl.ds(pl.multiple_of(core * hr + zz * zr, zr), zr)])
-    mine = pl.ds(pl.multiple_of(core * hr, hr), hr)
-    other = pl.ds(pl.multiple_of((1 - core) * hr, hr), hr)
-    a5 = send(lf.at[mine], lf.at[mine], m1)
-    chain(3)
-
-    wide = blk // 2
-
-    def product(slot, first):
-        def step(i, carry):
-            s = lax.div(i, 2)
-            cols = pl.ds(pl.multiple_of(lax.rem(i, 2) * wide, wide), wide)
-            value = dot_tn(tx[s, slot], cx[slot, :, cols])
-            if first:
-                acc[s, :, cols] = value
-            else:
-                acc[s, :, cols] = acc[s, :, cols] + value
-            return carry
-        return step
-
-    for s in (1, 2):
-        recv(tm[s, 0], tx.at[s, 0])
-    recv(tm[4, 0], tx.at[4, 0])
-    lax.fori_loop(0, 10, product(0, True), 0)
-
     recv(a5, lf.at[other])
     ex = {}
     for rel in (1, 3, 2, 0):
         q = lax.rem(x + rel, 4)
         gu = dot_tn(tq[q], lf[:, rank:2 * rank])
         ga = dot_tn(lf[:, 0:rank], cx[0, :, pl.ds(pl.multiple_of(q * qw, qw), qw)])
-        gb = dot_tn(lf[:, 0:rank], cx[0, :, pl.ds(pl.multiple_of(4 * qw + q * qw, qw), qw)])
+        gc = dot_tn(lf[:, 0:rank], cx[0, :, pl.ds(pl.multiple_of(4 * qw + q * qw, qw), qw)])
         if rel == 0:
             eo[0:2 * qw, :] = gu
             eo[2 * qw:2 * qw + rank, 0:qw] = ga
-            eo[2 * qw:2 * qw + rank, qw:2 * qw] = gb
+            eo[2 * qw:2 * qw + rank, qw:2 * qw] = gc
         else:
             eb[rel - 1, 0:2 * qw, :] = gu.astype(BF16)
             eb[rel - 1, 2 * qw:2 * qw + rank, 0:qw] = ga.astype(BF16)
-            eb[rel - 1, 2 * qw:2 * qw + rank, qw:2 * qw] = gb.astype(BF16)
+            eb[rel - 1, 2 * qw:2 * qw + rank, qw:2 * qw] = gc.astype(BF16)
             ex[rel] = send(eb.at[rel - 1], er.at[rel - 1], px(rel))
 
-    recv(xc[3, 1], cx.at[3, hi])
-    for s in (1, 2, 4):
-        recv(tm[s, 3], tx.at[s, 3])
-    lax.fori_loop(0, 10, product(3, False), 0)
-    recv(xc[1, 0], cx.at[1, lo])
-    for s in (1, 2, 4):
-        recv(tm[s, 1], tx.at[s, 1])
-    lax.fori_loop(0, 10, product(1, False), 0)
-    for s in (1, 2, 4):
+    for s in (1, 2):
         recv(tm[s, 2], tx.at[s, 2])
     recv(xf0, cx.at[2, lo])
     recv(xf1, cx.at[2, hi])
@@ -294,16 +292,27 @@
     home = pl.ds(pl.multiple_of(yh * qw, qw), qw)
     py = []
     last = product(2, False)
-    for s in range(5):
+
+    def close(s):
         last(2 * s, 0)
         last(2 * s + 1, 0)
         ps[s] = acc[s, away, :].astype(BF16)
         py.append(send(ps.at[s], pr.at[s], yy))
+
+    close(0)
+    close(1)
+    close(2)
+    close(3)
     for rel in (1, 3, 2):
         recv(ex[rel], er.at[rel - 1])
         eo[...] = eo[...] + er[rel - 1].astype(F32)
-    eu = send(eo.at[away], eyu, yy)
-    ev = send(eo.at[pl.ds(2 * qw, rank), away], eyv, yy)
+    su[...] = eo[away, :].astype(BF16)
+    sv[...] = eo[pl.ds(2 * qw, rank), away].astype(BF16)
+    eu = send(su, eyu, yy)
+    ev = send(sv, eyv, yy)
+    recv(tm[4, 2], tx.at[4, 2])
+    close(4)
+    chain(3)
 
     recv(t1, r1)
     recv(t2, r2)
@@ -324,12 +333,13 @@
     outs = [load(gt, gt_hbm)]
     for s in range(5):
         recv(py[s], pr.at[s])
-        acc[s, home, :] = (acc[s, home, :] + pr[s].astype(F32)) * scale
-        outs.append(load(acc.at[s, home, :], gb_hbm.at[s]))
+        value = (acc[s, home, :] + pr[s].astype(F32)) * scale
+        gb[s] = value.reshape(qw, 1, blk)
+        outs.append(load(gb.at[s], gb_hbm.at[:, s]))
     recv(eu, eyu)
     recv(ev, eyv)
-    gu_ref[...] = (eo[home, :] + eyu[...]) * scale
-    gv_ref[...] = (eo[pl.ds(2 * qw, rank), home] + eyv[...]) * scale
+    gu_ref[...] = (eo[home, :] + eyu[...].astype(F32)) * scale
+    gv_ref[...] = (eo[pl.ds(2 * qw, rank), home] + eyv[...].astype(F32)) * scale
     for cp in sent:
         cp.wait_send()
     for cp in outs:
@@ -359,6 +369,7 @@
         pltpu.VMEM((slots, qw, blk), BF16),
         pltpu.VMEM((slots, qw, blk), BF16),
         pltpu.VMEM(big, F32),
+        pltpu.VMEM((slots, qw, 1, blk), F32),
         pltpu.VMEM((rows, 2 * rank), F32),
         pltpu.VMEM((hr, 2 * rank), F32),
         pltpu.VMEM((3, hr // 4, 2 * rank), F32),
@@ -368,8 +379,10 @@
         pltpu.VMEM((3, 2 * qw + rank, rank), BF16),
         pltpu.VMEM((3, 2 * qw + rank, rank), BF16),
         pltpu.VMEM((2 * qw + rank, rank), F32),
-        pltpu.VMEM((qw, rank), F32),
-        pltpu.VMEM((rank, qw), F32),
+        pltpu.VMEM((qw, rank), BF16),
+        pltpu.VMEM((rank, qw), BF16),
+        pltpu.VMEM((qw, rank), BF16),
+        pltpu.VMEM((rank, qw), BF16),
         pltpu.SemaphoreType.DMA((32,)),
         pltpu.SemaphoreType.DMA((n_send,)),
         pltpu.SemaphoreType.DMA((n_send,)),
@@ -380,7 +393,7 @@
         functools.partial(kernel, rows, blk, rank, scale),
         out_shape=(
             jax.ShapeDtypeStruct(big, F32),
-            jax.ShapeDtypeStruct((slots, qw, blk), F32),
+            jax.ShapeDtypeStruct((qw, slots, 1, blk), F32),
             jax.ShapeDtypeStruct((qw, rank), F32),
             jax.ShapeDtypeStruct((rank, qw), F32),
         ),
@@ -392,7 +405,7 @@
         ),
         name="butterfly",
     )(tokens, cotangent, blocks_w[0], lowrank_u, lowrank_v)
-    return gt, jnp.transpose(gb, (1, 0, 2))[:, None], gu, gv
+    return gt, jnp.transpose(gb, (0, 2, 1, 3)), gu, gv
 
 
 def solution(mesh):

time: 147 us -> 126 us (0.86)
  Pallas kernels: 137 us -> 119 us
  local copies, waits for them, and re-layouts: 9.06 us -> 6.93 us
    pallas_call x1, Pallas kernels: 137 us -> 119 us  [per_device(): pl.pallas_call(functools.partial(kernel, rows, blk, rank, scale), out_sha...]
    unnamed x10, local copies, waits for them, and re-layouts: 9.06 us -> 6.93 us
where the time goes in v2:
time: 126 us
  Pallas kernels  119 us (94%)
  local copies, waits for them, and re-layouts  6.93 us (6%)
    pallas_call x1, Pallas kernels, per_device(): pl.pallas_call(functools.partial(kernel, rows, blk, rank, scale), out_sha...  119 us
    unnamed x10, local copies, waits for them, and re-layouts  6.93 us

profile of v2, /device:TPU:0, one launch (start us, length us, event | category | flops | bytes accessed | tf_op | source)
XLA Modules:
  0.0 126.2 jit_solution(2911516258798220218)
XLA Ops:
  0.6 118.6 %butterfly.1 = (f32[768,1024]{1,0:T(8,128)}, f32[128,5,1,1024]{3,2,1,0:T(1,128)}, f32[128,256]{1,0:T(8,128)}, f32[256,128]{1,0:T(8,128)}) custom-call(bf16[768,1024]{1,0:T(8,128)(2,1)} %tok_hbm.1, bf16[768,1024]{1,0:T(8,128)(2,1)} %cot_hbm.1, bf16[5,1024,1024]{2,1,0:T(8,128)(2,1)} %bitcast.2, bf16[1024,256]{1,0:T(8,128)(2,1)} %u_hbm.1, bf16[256,1024]{1,0:T(8,128)(2,1)} %v_hbm.1), custom_call_target="tpu_custom_call" | custom-call | tf_op jit(solution)/shard_map/butterfly/pallas_call | solution.py:392
  119.2 0.0 copy-start
  119.2 4.1 %copy.13 = f32[768,1024]{1,0:T(8,128)} copy(f32[768,1024]{1,0:T(8,128)} %get-tuple-element.16) | data formatting | bytes 6291456
  123.3 0.0 copy-done
  123.4 0.0 copy-start.2
  123.4 0.0 copy-start.1
  123.4 1.5 %copy.14 = f32[128,1,5,1024]{3,1,2,0:T(1,128)} copy(f32[128,1,5,1024]{3,1,2,0:T(1,128)S(1)} %bitcast.3) | data formatting | bytes 5242880
  124.8 0.0 copy-done.2
  124.9 0.7 copy.15
  125.5 0.0 copy-done.1
  125.5 0.7 copy.16
Async XLA Ops:
  119.2 4.1 %copy-start = (f32[128,5,1,1024]{3,2,1,0:T(1,128)S(1)}, f32[128,5,1,1024]{3,2,1,0:T(1,128)}, u32[]{:S(2)}) copy-start(f32[128,5,1,1024]{3,2,1,0:T(1,128)} %get-tuple-element.9) | copy-start | bytes 7864324
  123.4 1.5 %copy-start.2 = (f32[128,256]{1,0:T(8,128)S(1)}, f32[128,256]{1,0:T(8,128)}, u32[]{:S(2)}) copy-start(f32[128,256]{1,0:T(8,128)} %get-tuple-element.18) | copy-start | bytes 393220
  123.4 2.2 %copy-start.1 = (f32[256,128]{1,0:T(8,128)S(1)}, f32[256,128]{1,0:T(8,128)}, u32[]{:S(2)}) copy-start(f32[256,128]{1,0:T(8,128)} %get-tuple-element.19) | copy-start | bytes 393220

commit v3 on v2

--- a/solution.py
+++ b/solution.py
@@ -128,12 +128,13 @@
         xt[slot] = send(tq.at[lax.rem(x + rel, 4)], tx.at[0, slot], px(rel))
     cl.wait()
     half = rows // 2
+    wide = blk // 2
     lo, hi = pl.ds(0, half), pl.ds(half, half)
+    side = (pl.ds(0, wide), pl.ds(wide, wide))
     xc = {}
-    xc[3, 0] = send(cx.at[0, lo], cx.at[3, lo], px(1))
-    xc[1, 1] = send(cx.at[0, hi], cx.at[1, hi], px(3))
-    xc[3, 1] = send(cx.at[0, hi], cx.at[3, hi], px(1))
-    xc[1, 0] = send(cx.at[0, lo], cx.at[1, lo], px(3))
+    for g in range(2):
+        xc[3, g] = send(cx.at[0, :, side[g]], cx.at[3, :, side[g]], px(1))
+        xc[1, g] = send(cx.at[0, :, side[g]], cx.at[1, :, side[g]], px(3))
     wl = {s: load(w_hbm.at[s], w.at[s]) for s in (4, 2, 3, 1, 0)}
 
     ul.wait()
@@ -202,25 +203,29 @@
         term(3, s34, c * cr, cr, r4)
         t34.append(send(s34.at[at], r34.at[at], m4))
 
-    wide = blk // 2
-
-    def product(slot, first):
-        def step(i, carry):
-            s = lax.div(i, 2)
-            cols = pl.ds(pl.multiple_of(lax.rem(i, 2) * wide, wide), wide)
-            value = dot_tn(tx[s, slot], cx[slot, :, cols])
+    def product(slot, g, first):
+        def step(s, carry):
+            value = dot_tn(tx[s, slot], cx[slot, :, side[g]])
             if first:
-                acc[s, :, cols] = value
+                acc[s, :, side[g]] = value
             else:
-                acc[s, :, cols] = acc[s, :, cols] + value
+                acc[s, :, side[g]] = acc[s, :, side[g]] + value
             return carry
         return step
 
+    xf = {}
+
+    def pass_on(g):
+        recv(xc[3, g], cx.at[3, :, side[g]])
+        xf[0, g] = send(cx.at[3, lo, side[g]], cx.at[2, lo, side[g]], px(1))
+        recv(xc[1, g], cx.at[1, :, side[g]])
+        xf[1, g] = send(cx.at[1, hi, side[g]], cx.at[2, hi, side[g]], px(3))
 
     def multiply(slot, first):
         for s in (1, 2, 4):
             recv(tm[s, slot], tx.at[s, slot])
-        lax.fori_loop(0, 10, product(slot, first), 0)
+        for g in range(2):
+            lax.fori_loop(0, 5, product(slot, g, first), 0)
 
     for slot in (3, 1):
         recv(xt[slot], tx.at[0, slot])
@@ -250,23 +255,37 @@
         a4[v] = send(lf.at[piece], lf.at[piece], peer)
     fourth(2)
     wl[3].wait()
-    recv(xc[3, 0], cx.at[3, lo])
-    xf0 = send(cx.at[3, lo], cx.at[2, lo], px(1))
-    recv(xc[1, 1], cx.at[1, hi])
-    xf1 = send(cx.at[1, hi], cx.at[2, hi], px(3))
+    pass_on(0)
     chain(0)
     chain(1)
     onward(2)
     fourth(3)
     multiply(0, True)
-    recv(xc[3, 1], cx.at[3, hi])
+    pass_on(1)
     multiply(3, False)
-    recv(xc[1, 0], cx.at[1, lo])
     multiply(1, False)
+    away = pl.ds(pl.multiple_of((1 - yh) * qw, qw), qw)
+    home = pl.ds(pl.multiple_of(yh * qw, qw), qw)
+    py = {}
+
+    def close(s, g):
+        product(2, g, False)(s, 0)
+        ps[s, :, side[g]] = acc[s, away, side[g]].astype(BF16)
+        py[s, g] = send(ps.at[s, :, side[g]], pr.at[s, :, side[g]], yy)
+
+    for s in (1, 2):
+        recv(tm[s, 2], tx.at[s, 2])
     for v, peer in hops:
         recv(a4[v], lf.at[pl.ds(pl.multiple_of(core * hr + along(v) * zr, zr), zr)])
     a5 = send(lf.at[mine], lf.at[mine], m1)
-    chain(2)
+    for g in range(2):
+        recv(xf[0, g], cx.at[2, lo, side[g]])
+        recv(xf[1, g], cx.at[2, hi, side[g]])
+        for s in range(4):
+            close(s, g)
+    recv(tm[4, 2], tx.at[4, 2])
+    close(4, 0)
+    close(4, 1)
     recv(a5, lf.at[other])
     ex = {}
     for rel in (1, 3, 2, 0):
@@ -284,25 +303,8 @@
             eb[rel - 1, 2 * qw:2 * qw + rank, qw:2 * qw] = gc.astype(BF16)
             ex[rel] = send(eb.at[rel - 1], er.at[rel - 1], px(rel))
 
-    for s in (1, 2):
-        recv(tm[s, 2], tx.at[s, 2])
-    recv(xf0, cx.at[2, lo])
-    recv(xf1, cx.at[2, hi])
-    away = pl.ds(pl.multiple_of((1 - yh) * qw, qw), qw)
-    home = pl.ds(pl.multiple_of(yh * qw, qw), qw)
-    py = []
-    last = product(2, False)
-
-    def close(s):
-        last(2 * s, 0)
-        last(2 * s + 1, 0)
-        ps[s] = acc[s, away, :].astype(BF16)
-        py.append(send(ps.at[s], pr.at[s], yy))
-
-    close(0)
-    close(1)
-    close(2)
-    close(3)
+    chain(2)
+    chain(3)
     for rel in (1, 3, 2):
         recv(ex[rel], er.at[rel - 1])
         eo[...] = eo[...] + er[rel - 1].astype(F32)
@@ -310,9 +312,6 @@
     sv[...] = eo[pl.ds(2 * qw, rank), away].astype(BF16)
     eu = send(su, eyu, yy)
     ev = send(sv, eyv, yy)
-    recv(tm[4, 2], tx.at[4, 2])
-    close(4)
-    chain(3)
 
     recv(t1, r1)
     recv(t2, r2)
@@ -332,7 +331,8 @@
     lax.fori_loop(0, 4, total, 0)
     outs = [load(gt, gt_hbm)]
     for s in range(5):
-        recv(py[s], pr.at[s])
+        for g in range(2):
+            recv(py[s, g], pr.at[s, :, side[g]])
         value = (acc[s, home, :] + pr[s].astype(F32)) * scale
         gb[s] = value.reshape(qw, 1, blk)
         outs.append(load(gb.at[s], gb_hbm.at[:, s]))
@@ -354,7 +354,7 @@
     scale = 1.0 / math.sqrt(rows * lax.axis_size("dp"))
     big = (rows, blk)
     hr = rows // 2
-    n_send = 60
+    n_send = 64
     scratch = [
         pltpu.VMEM((4, rows, 2 * qw), BF16),
         pltpu.VMEM((4,) + big, BF16),

time: 126 us -> 126 us (level)
  no operation moved by 1% of the time
where the time goes in v3:
time: 126 us; the launch traced here: 125 us
  Pallas kernels  118 us (94%)
  local copies, waits for them, and re-layouts  6.93 us (6%)
    pallas_call x1, Pallas kernels, per_device(): pl.pallas_call(functools.partial(kernel, rows, blk, rank, scale), out_sha...  118 us
    unnamed x10, local copies, waits for them, and re-layouts  6.93 us

profile of v3, /device:TPU:0, one launch (start us, length us, event | category | flops | bytes accessed | tf_op | source)
XLA Modules:
  0.0 125.4 jit_solution(15744021731621501775)
XLA Ops:
  0.6 117.8 %butterfly.1 = (f32[768,1024]{1,0:T(8,128)}, f32[128,5,1,1024]{3,2,1,0:T(1,128)}, f32[128,256]{1,0:T(8,128)}, f32[256,128]{1,0:T(8,128)}) custom-call(bf16[768,1024]{1,0:T(8,128)(2,1)} %tok_hbm.1, bf16[768,1024]{1,0:T(8,128)(2,1)} %cot_hbm.1, bf16[5,1024,1024]{2,1,0:T(8,128)(2,1)} %bitcast.2, bf16[1024,256]{1,0:T(8,128)(2,1)} %u_hbm.1, bf16[256,1024]{1,0:T(8,128)(2,1)} %v_hbm.1), custom_call_target="tpu_custom_call" | custom-call | tf_op jit(solution)/shard_map/butterfly/pallas_call | solution.py:392
  118.5 0.0 copy-start
  118.5 4.1 %copy.13 = f32[768,1024]{1,0:T(8,128)} copy(f32[768,1024]{1,0:T(8,128)} %get-tuple-element.16) | data formatting | bytes 6291456
  122.6 0.0 copy-done
  122.6 0.0 copy-start.2
  122.6 0.0 copy-start.1
  122.6 1.5 %copy.14 = f32[128,1,5,1024]{3,1,2,0:T(1,128)} copy(f32[128,1,5,1024]{3,1,2,0:T(1,128)S(1)} %bitcast.3) | data formatting | bytes 5242880
  124.1 0.0 copy-done.2
  124.1 0.7 copy.15
  124.7 0.0 copy-done.1
  124.7 0.7 copy.16
Async XLA Ops:
  118.5 4.1 %copy-start = (f32[128,5,1,1024]{3,2,1,0:T(1,128)S(1)}, f32[128,5,1,1024]{3,2,1,0:T(1,128)}, u32[]{:S(2)}) copy-start(f32[128,5,1,1024]{3,2,1,0:T(1,128)} %get-tuple-element.9) | copy-start | bytes 7864324
  122.6 1.5 %copy-start.2 = (f32[128,256]{1,0:T(8,128)S(1)}, f32[128,256]{1,0:T(8,128)}, u32[]{:S(2)}) copy-start(f32[128,256]{1,0:T(8,128)} %get-tuple-element.18) | copy-start | bytes 393220
  122.6 2.2 %copy-start.1 = (f32[256,128]{1,0:T(8,128)S(1)}, f32[256,128]{1,0:T(8,128)}, u32[]{:S(2)}) copy-start(f32[256,128]{1,0:T(8,128)} %get-tuple-element.19) | copy-start | bytes 393220

commit v4 on v3

--- a/solution.py
+++ b/solution.py
@@ -236,12 +236,14 @@
     lz[...] = (
         lr1[pl.ds(pl.multiple_of(z * zr, zr), zr), :] + lr2[0] + lr2[1] + lr2[2]
     )
-    a3 = send(lz, lr3, m2)
+    yl = lax.rem(lax.div(mp, 2), 2)
+    hz = zr // 2
+    a3 = send(lz.at[pl.ds(pl.multiple_of((1 - yl) * hz, hz), hz)], lr3, m2)
     recv(xt[2], tx.at[0, 2])
     spread(2)
     wl[2].wait()
     term(2, s2, 0, rows)
-    t2 = send(s2, r2, m2)
+    t2 = [send(s2.at[lo], r2.at[lo], m2)]
     wl[1].wait()
     term(1, s1, 0, rows)
     t1 = send(s1, r1, m1)
@@ -249,10 +251,11 @@
     onward(1)
     recv(a3, lr3)
     piece = pl.ds(pl.multiple_of(core * hr + z * zr, zr), zr)
-    lf[piece, :] = (lz[...] + lr3[...]).astype(BF16)
-    a4 = {}
-    for v, peer in hops:
-        a4[v] = send(lf.at[piece], lf.at[piece], peer)
+    kept = pl.ds(pl.multiple_of(core * hr + z * zr + yl * hz, hz), hz)
+    given = pl.ds(pl.multiple_of(core * hr + z * zr + (1 - yl) * hz, hz), hz)
+    lf[kept, :] = (lz[pl.ds(pl.multiple_of(yl * hz, hz), hz), :] + lr3[...]).astype(BF16)
+    a6 = send(lf.at[kept], lf.at[kept], m2)
+    t2.append(send(s2.at[hi], r2.at[hi], m2))
     fourth(2)
     wl[3].wait()
     pass_on(0)
@@ -262,6 +265,10 @@
     fourth(3)
     multiply(0, True)
     pass_on(1)
+    recv(a6, lf.at[given])
+    a4 = {}
+    for v, peer in hops:
+        a4[v] = send(lf.at[piece], lf.at[piece], peer)
     multiply(3, False)
     multiply(1, False)
     away = pl.ds(pl.multiple_of((1 - yh) * qw, qw), qw)
@@ -275,14 +282,14 @@
 
     for s in (1, 2):
         recv(tm[s, 2], tx.at[s, 2])
-    for v, peer in hops:
-        recv(a4[v], lf.at[pl.ds(pl.multiple_of(core * hr + along(v) * zr, zr), zr)])
-    a5 = send(lf.at[mine], lf.at[mine], m1)
     for g in range(2):
         recv(xf[0, g], cx.at[2, lo, side[g]])
         recv(xf[1, g], cx.at[2, hi, side[g]])
         for s in range(4):
             close(s, g)
+    for v, peer in hops:
+        recv(a4[v], lf.at[pl.ds(pl.multiple_of(core * hr + along(v) * zr, zr), zr)])
+    a5 = send(lf.at[mine], lf.at[mine], m1)
     recv(tm[4, 2], tx.at[4, 2])
     close(4, 0)
     close(4, 1)
@@ -314,7 +321,8 @@
     ev = send(sv, eyv, yy)
 
     recv(t1, r1)
-    recv(t2, r2)
+    recv(t2[0], r2.at[lo])
+    recv(t2[1], r2.at[hi])
     for c in range(CHUNKS):
         recv(t34[c], r34.at[pl.ds(c * cr, cr)])
     wl[0].wait()
@@ -374,7 +382,7 @@
         pltpu.VMEM((hr, 2 * rank), F32),
         pltpu.VMEM((3, hr // 4, 2 * rank), F32),
         pltpu.VMEM((hr // 4, 2 * rank), F32),
-        pltpu.VMEM((hr // 4, 2 * rank), F32),
+        pltpu.VMEM((hr // 8, 2 * rank), F32),
         pltpu.VMEM((rows, 2 * rank), BF16),
         pltpu.VMEM((3, 2 * qw + rank, rank), BF16),
         pltpu.VMEM((3, 2 * qw + rank, rank), BF16),

time: 126 us -> 130 us (1.032)
  Pallas kernels: 118 us -> 121 us
    pallas_call x1, Pallas kernels: 118 us -> 121 us  [per_device(): pl.pallas_call(functools.partial(kernel, rows, blk, rank, scale), out_sha...]
where the time goes in v4:
time: 130 us; the launch traced here: 128 us
  Pallas kernels  121 us (93%)
  local copies, waits for them, and re-layouts  6.93 us (5%)
    pallas_call x1, Pallas kernels, per_device(): pl.pallas_call(functools.partial(kernel, rows, blk, rank, scale), out_sha...  121 us
    unnamed x10, local copies, waits for them, and re-layouts  6.93 us

profile of v4, /device:TPU:0, one launch (start us, length us, event | category | flops | bytes accessed | tf_op | source)
XLA Modules:
  0.0 128.3 jit_solution(2421222166679916885)
XLA Ops:
  0.6 120.8 %butterfly.1 = (f32[768,1024]{1,0:T(8,128)}, f32[128,5,1,1024]{3,2,1,0:T(1,128)}, f32[128,256]{1,0:T(8,128)}, f32[256,128]{1,0:T(8,128)}) custom-call(bf16[768,1024]{1,0:T(8,128)(2,1)} %tok_hbm.1, bf16[768,1024]{1,0:T(8,128)(2,1)} %cot_hbm.1, bf16[5,1024,1024]{2,1,0:T(8,128)(2,1)} %bitcast.2, bf16[1024,256]{1,0:T(8,128)(2,1)} %u_hbm.1, bf16[256,1024]{1,0:T(8,128)(2,1)} %v_hbm.1), custom_call_target="tpu_custom_call" | custom-call | tf_op jit(solution)/shard_map/butterfly/pallas_call | solution.py:400
  121.4 0.0 copy-start
  121.4 4.1 %copy.13 = f32[768,1024]{1,0:T(8,128)} copy(f32[768,1024]{1,0:T(8,128)} %get-tuple-element.16) | data formatting | bytes 6291456
  125.5 0.0 copy-done
  125.5 0.0 copy-start.2
  125.5 0.0 copy-start.1
  125.5 1.5 %copy.14 = f32[128,1,5,1024]{3,1,2,0:T(1,128)} copy(f32[128,1,5,1024]{3,1,2,0:T(1,128)S(1)} %bitcast.3) | data formatting | bytes 5242880
  127.0 0.0 copy-done.2
  127.0 0.7 copy.15
  127.7 0.0 copy-done.1
  127.7 0.7 copy.16
Async XLA Ops:
  121.4 4.1 %copy-start = (f32[128,5,1,1024]{3,2,1,0:T(1,128)S(1)}, f32[128,5,1,1024]{3,2,1,0:T(1,128)}, u32[]{:S(2)}) copy-start(f32[128,5,1,1024]{3,2,1,0:T(1,128)} %get-tuple-element.9) | copy-start | bytes 7864324
  125.5 1.5 %copy-start.2 = (f32[128,256]{1,0:T(8,128)S(1)}, f32[128,256]{1,0:T(8,128)}, u32[]{:S(2)}) copy-start(f32[128,256]{1,0:T(8,128)} %get-tuple-element.18) | copy-start | bytes 393220
  125.5 2.2 %copy-start.1 = (f32[256,128]{1,0:T(8,128)S(1)}, f32[256,128]{1,0:T(8,128)}, u32[]{:S(2)}) copy-start(f32[256,128]{1,0:T(8,128)} %get-tuple-element.19) | copy-start | bytes 393220
